TPU v7x, 1024 devices: a whole 4x4x32 slice. The times are simulated.
1024 devices in a mesh: pipe: 16 (over z_lo), ctx: 8 (over z_hi, x), tp: 8 (over y, core).
Axes of the slice: x: 4, y: 4, z: 32 (z_hi: 2, z_lo: 16; z = z_hi * 16 + z_lo), core: 2. Of those that a mesh axis runs over, the one named last changes fastest.
Arguments:
- inputs: bfloat16 [16, 2048, 5120], P('pipe', ('ctx', 'tp')), may hold values from -6 to 6
- doc_lengths: int32 [16, 8], P('pipe'), may hold values from 1 to 1024, 2048 in all within a row
- w_query: bfloat16 [16, 5120, 3072], P('pipe', None, 'tp'), may hold values from -0.078125 to 0.078125
- w_key: bfloat16 [16, 5120, 1024], P('pipe', 'ctx', 'tp'), may hold values from -0.078125 to 0.078125
- w_value: bfloat16 [16, 5120, 1024], P('pipe', 'ctx', 'tp'), may hold values from -0.078125 to 0.078125
- w_out: bfloat16 [16, 3072, 5120], P('pipe', 'tp'), may hold values from -0.625 to 0.625
Outputs:
- next_input: bfloat16 [16, 2048, 5120], P('pipe', ('ctx', 'tp'))
Inputs may be any that keep to these rules, and one draw needn't show every extreme that they name: `doc_lengths`: the 8 lengths of a micro-batch sum to 2048; the longest is exactly 1024.
All inputs are finite; a program needn't handle non-finite values.
Results may differ from a plain program's by a relative error of at most 0.015.
Values may be sent and summed in bfloat16 or wider, within the bound.
A program may use at most 64 MiB of HBM per device.

v0:
```python
import jax
import jax.numpy as jnp
from jax import lax
from jax.sharding import PartitionSpec as P

HD = 128
SPAN = 1024


ROPE_BASE = 500000.0
NORM_EPS = 1e-06


def from_behind(value, axis, steps):
    count = lax.axis_size(axis)
    pairs = [(source, (source + steps) % count) for source in range(count)]
    return lax.ppermute(value, axis, pairs)


def doc_index(positions, lengths):
    doc_ends = jnp.cumsum(lengths)
    return jnp.sum((positions[:, None] >= doc_ends[None, :]).astype(jnp.int32), axis=1)


def norm_rotate(entries, positions, head_count, head_width):
    row_count = entries.shape[0]
    shaped = entries.reshape(row_count, head_count, head_width)
    shaped = shaped * lax.rsqrt(jnp.mean(shaped * shaped, axis=-1, keepdims=True) + NORM_EPS)
    half_width = head_width // 2
    frequencies = jnp.power(
        ROPE_BASE, -(jnp.arange(half_width, dtype=jnp.float32) * 2.0 / head_width)
    )
    angles = positions.astype(jnp.float32)[:, None] * frequencies[None, :]
    cosine = jnp.cos(angles)[:, None, :]
    sine_part = jnp.sin(angles)[:, None, :]
    first_half = shaped[..., :half_width]
    second = shaped[..., half_width:]
    turned = jnp.concatenate(
        [first_half * cosine - second * sine_part, second * cosine + first_half * sine_part],
        axis=-1,
    )
    return turned.reshape(row_count, head_count * head_width)


def attend(queries, q_pos, q_doc, key_rows, value_rows, k_pos, k_doc):
    score_scale = 1.0 / HD**0.5
    scores = (
        jnp.einsum("tkgd,nkd->kgtn", queries, key_rows, preferred_element_type=jnp.float32)
        * score_scale
    )
    allowed = (
        (k_pos[None, :] <= q_pos[:, None])
        & (k_doc[None, :] == q_doc[:, None])
        & (k_pos[None, :] // SPAN == q_pos[:, None] // SPAN)
    )
    weights = jnp.where(allowed[None, None], jnp.exp(scores), 0.0).astype(jnp.bfloat16)
    numerator = jnp.einsum(
        "kgtn,nkd->tkgd", weights, value_rows, preferred_element_type=jnp.float32
    )
    denominator = jnp.sum(weights.astype(jnp.float32), axis=-1)
    return (numerator, denominator)


def on_device(inputs, doc_lengths, w_query, w_key, w_value, w_out):
    tok_rows = lax.all_gather(inputs[0], "tp", axis=0, tiled=True)
    block_rows = tok_rows.shape[0]
    q_heads = w_query.shape[2] // HD
    kv_heads = w_key.shape[2] // HD
    group_size = q_heads // kv_heads
    ctx_rank = lax.axis_index("ctx")
    positions = ctx_rank * block_rows + jnp.arange(block_rows, dtype=jnp.int32)
    lengths = doc_lengths[0]
    own_docs = doc_index(positions, lengths)
    queries = jnp.dot(tok_rows, w_query[0], preferred_element_type=jnp.float32)
    stacked_weights = jnp.stack([w_key[0], w_value[0]])
    key_value = jnp.einsum(
        "td,sdc->stc",
        tok_rows,
        lax.all_gather(stacked_weights, "ctx", axis=1, tiled=True),
        preferred_element_type=jnp.float32,
    )
    keys_float = key_value[0]
    values_float = key_value[1]
    q_round = (
        norm_rotate(queries, positions, q_heads, HD)
        .astype(jnp.bfloat16)
        .reshape(block_rows, kv_heads, group_size, HD)
    )
    k_round = norm_rotate(keys_float, positions, kv_heads, HD).astype(jnp.bfloat16)
    v_round = values_float.astype(jnp.bfloat16)
    key_value_pair = jnp.stack([k_round, v_round])
    shard_piece = lax.all_gather(key_value_pair, "ctx", axis=1, tiled=True)
    row_count = shard_piece.shape[1]
    k_pos = jnp.arange(row_count, dtype=jnp.int32)
    k_doc = doc_index(k_pos, lengths)
    key_rows = shard_piece[0].reshape(row_count, kv_heads, HD)
    value_rows = shard_piece[1].reshape(row_count, kv_heads, HD)
    numerator, denominator = attend(
        q_round, positions, own_docs, key_rows, value_rows, k_pos, k_doc
    )
    attended = (
        (numerator / jnp.transpose(denominator, (2, 0, 1))[..., None])
        .astype(jnp.bfloat16)
        .reshape(block_rows, q_heads * HD)
    )
    mixed = lax.psum_scatter(
        jnp.dot(attended, w_out[0], preferred_element_type=jnp.float32).astype(jnp.bfloat16),
        "tp",
        scatter_dimension=0,
        tiled=True,
    )
    received = from_behind(mixed, "pipe", 1)
    return received[None]


def solution(mesh):
    in_specs = (
        P("pipe", ("ctx", "tp"), None),
        P("pipe", None),
        P("pipe", None, "tp"),
        P("pipe", "ctx", "tp"),
        P("pipe", "ctx", "tp"),
        P("pipe", "tp", None),
    )
    out_specs = P("pipe", ("ctx", "tp"), None)
    return jax.shard_map(
        on_device, mesh=mesh, in_specs=in_specs, out_specs=out_specs, check_vma=False
    )
```

profile of v0, /device:TPU:2, one launch (start us, length us, event | category | flops | bytes accessed | tf_op | source)
XLA Modules:
  0.0 513.3 jit_solution(12323157934383462381)
XLA Ops:
  6.5 0.7 all-gather.9.cloned.1.call-update
  7.3 0.0 all-gather.5.cloned.1.call-start
  7.3 1.1 copy.20
  8.4 1.1 copy.19
  9.4 0.8 pad_maximum_fusion
  10.2 0.0 all-gather.5.cloned.1.call-update
  10.2 0.0 all-gather.7.cloned.1.call-start
  10.3 6.3 %copy.21 = bf16[1,5120,384]{1,2,0:T(8,128)(2,1)} copy(bf16[1,5120,384]{2,1,0:T(8,128)(2,1)} %param.8) | data formatting | bytes 7864320 | tf_op args[2]
  16.6 0.2 reduce-window.8
  16.8 0.1 convert_reduce_fusion.1
  16.9 0.1 convert_reduce_fusion.2
  17.0 44.6 %all-gather.9.cloned.1.call-done = bf16[1,256,5120]{2,1,0:T(8,128)(2,1)} async-done(((bf16[1,32,5120]{2,1,0:T(8,128)(2,1)}), bf16[1,256,5120]{2,1,0:T(8,128)(2,1)}) %all-gather.9.cloned.1.call-update) | async-done | bytes 2621456 | tf_op jit(solution)/shard_map/all_gather | solution.py:65
  61.6 189.7 %all-gather.5.cloned.1.call-done = bf16[2,5120,128]{1,2,0:T(8,128)(2,1)} async-done(((bf16[2,640,128]{1,2,0:T(8,128)(2,1)}), bf16[2,5120,128]{1,2,0:T(8,128)(2,1)}) %all-gather.5.cloned.1.call-update) | async-done | bytes 2621456 | tf_op jit(solution)/shard_map/all_gather | solution.py:79
  251.4 3.4 fusion.13
  254.9 0.3 fusion.31
  255.2 0.7 pad_maximum_fusion.1
  255.9 0.0 all-gather.7.cloned.1.call-update
  255.9 0.0 reduce-scatter.2.cloned.1.call-start
  255.9 0.3 multiply_cosine_fusion
  256.3 1.4 fusion.9
  257.7 3.3 multiply_reduce_fusion
  261.1 0.1 subtract_convert_fusion
  261.2 177.0 %all-gather.7.cloned.1.call-done = bf16[2,2048,128]{1,2,0:T(8,128)(2,1)} async-done(((bf16[2,256,128]{1,2,0:T(8,128)(2,1)}), bf16[2,2048,128]{1,2,0:T(8,128)(2,1)}) %all-gather.7.cloned.1.call-update) | async-done | bytes 1048592 | tf_op jit(solution)/shard_map/all_gather | solution.py:92
  438.2 2.8 convert_reduce_fusion
  441.0 0.6 fusion.19
  441.6 1.5 copy-done
  443.1 3.1 convolution_convert_fusion
  446.1 0.0 reduce-scatter.2.cloned.1.call-update
  446.2 33.7 %reduce-scatter.2.cloned.1.call-done = bf16[32,5120]{1,0:T(8,128)(2,1)} async-done(((bf16[256,5120]{1,0:T(8,128)(2,1)}), bf16[32,5120]{1,0:T(8,128)(2,1)}) %reduce-scatter.2.cloned.1.call-update) | async-done | bytes 327696 | tf_op jit(solution)/shard_map/reduce_scatter | solution.py:106
  479.9 3.4 collective-permute-start
  483.3 22.8 %collective-permute-done = bf16[32,5120]{1,0:T(8,128)(2,1)S(1)} collective-permute-done((bf16[32,5120]{1,0:T(8,128)(2,1)}, bf16[32,5120]{1,0:T(8,128)(2,1)S(1)}, u32[]{:S(2)}, u32[]{:S(2)}) %collective-permute-start) | collective-permute-done | bytes 327712 | tf_op jit(solution)/shard_map/ppermute | solution.py:17
  506.1 0.7 copy.30
  (19 shorter events, 0.2 us)
Async XLA Ops:
  6.5 55.1 %all-gather.9.cloned.1.call-start = ((), (), s32[]{:S(2)}) async-start(), calls=%async_computation.4 | async-start | bytes 2949120 | tf_op jit(solution)/shard_map/all_gather | solution.py:65
  7.3 244.1 %all-gather.5.cloned.1.call-start = ((), (), s32[]{:S(2)}) async-start(), calls=%async_computation.1 | async-start | bytes 2949120 | tf_op jit(solution)/shard_map/all_gather | solution.py:79
  10.2 428.0 %all-gather.7.cloned.1.call-start = ((), (), s32[]{:S(2)}) async-start(), calls=%async_computation.2 | async-start | bytes 1179648 | tf_op jit(solution)/shard_map/all_gather | solution.py:92
  10.3 6.3 %copy-start.3 = (s32[1,8]{1,0:T(1,128)S(1)}, s32[1,8]{1,0:T(1,128)}, u32[]{:S(2)}) copy-start(s32[1,8]{1,0:T(1,128)} %param.7) | copy-start | bytes 100
  61.6 196.1 %copy-start.1 = (bf16[1,256,5120]{2,1,0:T(8,128)(2,1)S(1)}, bf16[1,256,5120]{2,1,0:T(8,128)(2,1)}, u32[]{:S(2)}) copy-start(bf16[1,256,5120]{2,1,0:T(8,128)(2,1)} %all-gather.9.cloned.1.call-done) | copy-start | bytes 7864324
  255.9 224.0 %reduce-scatter.2.cloned.1.call-start = ((), (), s32[]{:S(2)}) async-start(), calls=%async_computation.3 | async-start | bytes 2949120 | tf_op jit(solution)/shard_map/reduce_scatter | solution.py:106
  438.2 2.8 copy-start.2
  441.0 2.1 copy-start
  479.9 26.2 %collective-permute-start = (bf16[32,5120]{1,0:T(8,128)(2,1)}, bf16[32,5120]{1,0:T(8,128)(2,1)S(1)}, u32[]{:S(2)}, u32[]{:S(2)}) collective-permute-start(bf16[32,5120]{1,0:T(8,128)(2,1)} %reduce-scatter.2.cloned.1.call-done), channel_id=1, source_target_pairs={{0,64},{64,128},{128,192},{192,256},{256,320},{320,384},{384,448},... | collective-permute-start | bytes 983048 | tf_op jit(solution)/shard_map/ppermute | solution.py:17
Sparse Core Ops, SparseCore 0:
  10.1 51.5 all-gather.8
  66.0 185.3 all-gather.4
  256.0 182.1 all-gather.6
  446.3 33.5 reduce-scatter.1
where the time goes:
time: 514 us; the launch traced here: 513 us
  waiting for transfers between devices  469 us (91%)
  between operations  13.3 us (3%)
  matrix products  13.2 us (3%)
  local copies, waits for them, and re-layouts  10.7 us (2%)
    all_gather x1, waiting for transfers between devices, on_device(): lax.all_gather(stacked_weights, 'ctx', axis=1, tiled=True)  190 us
    all_gather x1, waiting for transfers between devices, on_device(): shard_piece = lax.all_gather(key_value_pair, 'ctx', axis=1, tiled=True)  177 us
    all_gather x1, waiting for transfers between devices, on_device(): tok_rows = lax.all_gather(inputs[0], 'tp', axis=0, tiled=True)  44.6 us
    reduce_scatter x1, waiting for transfers between devices, on_device(): lax.psum_scatter(jnp.dot(attended, w_out[0], preferred_element_type=jnp.f...  33.7 us
    ppermute x1, waiting for transfers between devices, from_behind(): return lax.ppermute(value, axis, pairs)  22.8 us
    unnamed x12, local copies, waits for them, and re-layouts  10.7 us
  transfers between devices with their start and end apart: 5, of which 5 were waited for; matrix products, arithmetic and copies ran while one was open for 3% of the time, Pallas kernels for 0%

commit v1 on v0

v1 whole, which is shorter than its diff:
```python
import functools

import jax
import jax.numpy as jnp
import numpy as np
from jax import lax
from jax.experimental import pallas as pl
from jax.experimental.pallas import tpu as pltpu
from jax.sharding import PartitionSpec as P

HD = 128
ROPE_BASE = 500000.0
NORM_EPS = 1e-06
ROWS = 128
PIECES = 4
NEG = -1e30
MESH = pl.DeviceIdType.MESH


def layer_kernel(
    sizes,
    x_ref, len_ref, freq_ref, wq_ref, wk_ref, wv_ref, wo_ref,
    o_ref,
    tok, wq, wo, wk, wv, q_acc, qr, kv_acc, kvb, mask, cosb, sinb, acc, att,
    part, recv_a, pair, recv_b, outb,
    l_sem, z_s, z_r, t_s, t_r, own_s, own_r, fwd_s, fwd_r, kv_s, kv_r,
    a_s, a_r, b_s, b_r, c_s, c_r,
):
    NP, X, Y = sizes
    TP = 2 * Y
    TR, D = x_ref.shape
    TB = TR * TP
    RB = wk_ref.shape[0]
    QW = wq_ref.shape[1]
    G = QW // HD
    NCH = RB // ROWS
    CW = D // PIECES

    pipe, ctx, t = lax.axis_index("pipe"), lax.axis_index("ctx"), lax.axis_index("tp")
    zhi, x = ctx // X, ctx % X
    y, c = t // 2, t % 2

    z_dev = (pipe, (1 - zhi) * X + x, t)
    next_dev = ((pipe + 1) % NP, ctx, t)
    prev_dev = ((pipe + NP - 1) % NP, ctx, t)
    core_dev = (pipe, ctx, y * 2 + 1 - c)

    def flip(i, r, n):
        out = 0
        bit = 1
        while bit < n:
            b = (i // bit) % 2
            out = out + bit * ((1 - b) if (r // bit) % 2 else b)
            bit *= 2
        return out

    def x_dev(xx):
        return (pipe, zhi * X + xx, t)

    def copy(src, dst, ss, rs, dev):
        return pltpu.make_async_remote_copy(
            src_ref=src, dst_ref=dst, send_sem=ss, recv_sem=rs, device_id=dev, device_id_type=MESH
        )

    def rows(start, n):
        return pl.ds(pl.multiple_of(start, n), n)

    mine = ctx * RB
    theirs = ((1 - zhi) * X + x) * RB

    locals_ = [
        pltpu.make_async_copy(x_ref, tok.at[rows(t * TR, TR)], l_sem.at[0]),
        pltpu.make_async_copy(wk_ref, wk.at[rows(mine, ROWS * NCH)], l_sem.at[1]),
        pltpu.make_async_copy(wv_ref, wv.at[rows(mine, ROWS * NCH)], l_sem.at[2]),
        pltpu.make_async_copy(wq_ref, wq, l_sem.at[3]),
        pltpu.make_async_copy(wo_ref, wo, l_sem.at[4]),
    ]
    for cp in locals_:
        cp.start()

    barrier = pltpu.get_barrier_semaphore()
    friends = [z_dev, next_dev, prev_dev]
    friends += [x_dev(flip(x, r, X)) for r in range(1, X)]
    friends += [(pipe, ctx, flip(t, r, TP)) for r in range(1, TP)]
    for dev in friends:
        pl.semaphore_signal(barrier, inc=1, device_id=dev, device_id_type=MESH)
    pl.semaphore_wait(barrier, len(friends))

    def z_copy(j, i, base):
        src = (wk_ref, wv_ref)[i].at[pl.ds(j * ROWS, ROWS)]
        dst = (wk, wv)[i].at[rows(base + j * ROWS, ROWS)]
        return copy(src, dst, z_s.at[j, i], z_r.at[j, i], z_dev)

    for j in range(NCH):
        for i in range(2):
            z_copy(j, i, mine).start()

    def tok_copy(r, who):
        return copy(x_ref, tok.at[rows(who * TR, TR)], t_s.at[r - 1], t_r.at[r - 1], (pipe, ctx, flip(t, r, TP)))

    for r in range(1, TP):
        tok_copy(r, t).start()

    def own_copy(r, i, xx):
        dst = (wk, wv)[i].at[rows((zhi * X + xx) * RB, ROWS * NCH)]
        return copy((wk_ref, wv_ref)[i], dst, own_s.at[r - 1, i], own_r.at[r - 1, i], x_dev(flip(x, r, X)))

    for r in range(1, X):
        for i in range(2):
            own_copy(r, i, x).start()

    first = ctx * TB
    row_pos = lax.broadcasted_iota(jnp.int32, (TB, HD), 0) + first
    angle = row_pos.astype(jnp.float32) * freq_ref[0:1, :]
    cosb[...] = jnp.cos(angle)
    lane = lax.broadcasted_iota(jnp.int32, (TB, HD), 1)
    sine = jnp.sin(angle)
    sinb[...] = jnp.where(lane < HD // 2, -sine, sine)

    n_docs = len_ref.shape[1]
    ends = []
    total = 0
    for m in range(n_docs):
        total = total + len_ref[0, m]
        ends.append(total)
    q_pos = lax.broadcasted_iota(jnp.int32, (TB, TB), 0) + first
    q_doc = sum((q_pos >= e).astype(jnp.int32) for e in ends)
    for d in range(X):
        k_pos = lax.broadcasted_iota(jnp.int32, (TB, TB), 1) + (first - d * TB)
        k_doc = sum((k_pos >= e).astype(jnp.int32) for e in ends)
        mask[d] = jnp.where((k_pos <= q_pos) & (k_doc == q_doc), 0.0, NEG)

    def norm_rotate(head):
        scaled = head * lax.rsqrt(jnp.mean(head * head, axis=-1, keepdims=True) + NORM_EPS)
        return (scaled * cosb[...] + pltpu.roll(scaled, HD // 2, 1) * sinb[...]).astype(jnp.bfloat16)

    locals_[0].wait()
    for r in range(1, TP):
        tok_copy(r, flip(t, r, TP)).wait_recv()
    locals_[3].wait()
    q_acc[...] = jnp.zeros_like(q_acc)
    QK = D // (2 * X)

    def q_step(i, carry):
        s = rows(i * QK, QK)
        q_acc[...] += jnp.dot(tok[:, s], wq[s, :], preferred_element_type=jnp.float32)
        return carry

    lax.fori_loop(0, 2 * X, q_step, 0)
    for h in range(G):
        qr[pl.ds(h * TB, TB), :] = norm_rotate(q_acc[:, h * HD : (h + 1) * HD])

    locals_[1].wait()
    locals_[2].wait()
    for r in range(1, X):
        for i in range(2):
            own_copy(r, i, flip(x, r, X)).wait_recv()
    kv_acc[...] = jnp.zeros_like(kv_acc)

    def kv_add(start, n):
        s = rows(start, n)
        left = tok[:, s]
        kv_acc[0] += jnp.dot(left, wk[s, :], preferred_element_type=jnp.float32)
        kv_acc[1] += jnp.dot(left, wv[s, :], preferred_element_type=jnp.float32)

    def kv_step(i, carry):
        kv_add((zhi * X + i) * RB, ROWS * NCH)
        return carry

    lax.fori_loop(0, X, kv_step, 0)

    def fwd_copy(j, r, i, base):
        ref = (wk, wv)[i].at[rows(base + j * ROWS, ROWS)]
        return copy(ref, ref, fwd_s.at[j, r - 1, i], fwd_r.at[j, r - 1, i], x_dev(flip(x, r, X)))

    def peer_base(r):
        return ((1 - zhi) * X + flip(x, r, X)) * RB

    def take_chunk(j):
        kv_add(theirs + j * ROWS, ROWS)
        for r in range(1, X):
            for i in range(2):
                fwd_copy(j, r, i, peer_base(r)).wait_recv()
            kv_add(peer_base(r) + j * ROWS, ROWS)

    for j in range(NCH):
        for i in range(2):
            z_copy(j, i, theirs).wait_recv()
        for r in range(1, X):
            for i in range(2):
                fwd_copy(j, r, i, theirs).start()
        if j:
            take_chunk(j - 1)
    take_chunk(NCH - 1)

    kvb[0, 0] = norm_rotate(kv_acc[0])
    kvb[0, 1] = kv_acc[1].astype(jnp.bfloat16)

    def kv_copy(d, xx):
        return copy(kvb.at[0], kvb.at[d], kv_s.at[d - 1], kv_r.at[d - 1], x_dev(xx))

    for d in range(1, X):

        @pl.when(x + d < X)
        def _(d=d):
            kv_copy(d, x + d).start()

    scale = 1.0 / HD**0.5
    ones = jnp.ones((TB, HD), jnp.bfloat16)

    def attend(d):
        s = lax.dot_general(
            qr[...], kvb[d, 0], (((1,), (1,)), ((), ())), preferred_element_type=jnp.float32
        )
        s = s.reshape(G, TB, TB) * scale + mask[d][None]
        e = jnp.exp(s).astype(jnp.bfloat16).reshape(G * TB, TB)
        return jnp.dot(
            e, jnp.concatenate([kvb[d, 1], ones], axis=1), preferred_element_type=jnp.float32
        )

    acc[...] = attend(0)
    for d in range(1, X):

        @pl.when(x >= d)
        def _(d=d):
            kv_copy(d, x - d).wait_recv()
            acc[...] += attend(d)

    for h in range(G):
        block = acc[pl.ds(h * TB, TB), :]
        att[:, h * HD : (h + 1) * HD] = (block[:, :HD] / block[:, HD:]).astype(jnp.bfloat16)

    locals_[4].wait()

    def a_copy(k):
        return copy(part.at[k, 1 - c], recv_a.at[k], a_s.at[k], a_r.at[k], core_dev)

    def b_copy(k, r):
        yy = flip(y, r, Y)
        return copy(pair.at[k, yy], recv_b.at[k, r - 1], b_s.at[k, r - 1], b_r.at[k, r - 1], (pipe, ctx, yy * 2 + c))

    def c_copy(k):
        return copy(outb.at[k], o_ref.at[:, rows(k * CW, CW)], c_s.at[k], c_r.at[k], next_dev)

    def project(k, carry):
        product = jnp.dot(
            att[...], wo[:, rows(k * CW, CW)], preferred_element_type=jnp.float32
        ).astype(jnp.bfloat16)
        for who in range(TP):
            part[k, who % 2, who // 2] = product[who * TR : (who + 1) * TR]
        a_copy(k).start()
        return carry

    lax.fori_loop(0, PIECES, project, 0)

    def pair_sum(k, carry):
        a_copy(k).wait_recv()
        pair[k] = (part[k, c].astype(jnp.float32) + recv_a[k].astype(jnp.float32)).astype(jnp.bfloat16)
        for r in range(Y - 1, 0, -1):
            b_copy(k, r).start()
        return carry

    lax.fori_loop(0, PIECES, pair_sum, 0)

    def last_sum(k, carry):
        whole = part[k, c, y].astype(jnp.float32) + recv_a[k, y].astype(jnp.float32)
        for r in range(1, Y):
            b_copy(k, r).wait_recv()
            whole = whole + recv_b[k, r - 1].astype(jnp.float32)
        outb[k] = whole.astype(jnp.bfloat16)
        c_copy(k).start()
        return carry

    lax.fori_loop(0, PIECES, last_sum, 0)

    for j in range(NCH):
        for i in range(2):
            z_copy(j, i, mine).wait_send()
            for r in range(1, X):
                fwd_copy(j, r, i, theirs).wait_send()
    for r in range(1, TP):
        tok_copy(r, t).wait_send()
    for r in range(1, X):
        for i in range(2):
            own_copy(r, i, x).wait_send()
    for d in range(1, X):

        @pl.when(x + d < X)
        def _(d=d):
            kv_copy(d, x + d).wait_send()

    def drain(k, carry):
        a_copy(k).wait_send()
        for r in range(1, Y):
            b_copy(k, r).wait_send()
        c_copy(k).wait_send()
        c_copy(k).wait_recv()
        return carry

    lax.fori_loop(0, PIECES, drain, 0)


def solution(mesh):
    NP, X, Y = mesh.shape["pipe"], mesh.shape["ctx"] // 2, mesh.shape["tp"] // 2

    def on_device(inputs, doc_lengths, w_query, w_key, w_value, w_out):
        TR, D = inputs.shape[1:]
        TB = TR * 2 * Y
        RB, QW = w_key.shape[1], w_query.shape[2]
        G, NCH, CW = QW // HD, RB // ROWS, D // PIECES
        half = np.arange(HD // 2, dtype=np.float32) * np.float32(2.0) / np.float32(HD)
        freq = np.power(np.float32(ROPE_BASE), -half).astype(np.float32)
        freq = jnp.asarray(np.tile(np.concatenate([freq, freq])[None], (8, 1)))
        bf, f32 = jnp.bfloat16, jnp.float32
        vmem, dma = pltpu.VMEM, pltpu.SemaphoreType.DMA
        hbm = pl.BlockSpec(memory_space=pl.ANY)
        out = pl.pallas_call(
            functools.partial(layer_kernel, (NP, X, Y)),
            out_shape=jax.ShapeDtypeStruct((TR, D), bf),
            in_specs=[
                hbm,
                pl.BlockSpec(memory_space=pltpu.SMEM),
                pl.BlockSpec(memory_space=pltpu.VMEM),
                hbm, hbm, hbm, hbm,
            ],
            out_specs=hbm,
            scratch_shapes=[
                vmem((TB, D), bf), vmem((D, QW), bf), vmem((QW, D), bf), vmem((D, HD), bf), vmem((D, HD), bf),
                vmem((TB, QW), f32), vmem((G * TB, HD), bf), vmem((2, TB, HD), f32), vmem((X, 2, TB, HD), bf),
                vmem((X, TB, TB), f32), vmem((TB, HD), f32), vmem((TB, HD), f32), vmem((G * TB, 2 * HD), f32),
                vmem((TB, QW), bf),
                vmem((PIECES, 2, Y, TR, CW), bf), vmem((PIECES, Y, TR, CW), bf), vmem((PIECES, Y, TR, CW), bf),
                vmem((PIECES, Y - 1, TR, CW), bf), vmem((PIECES, TR, CW), bf),
                dma((5,)), dma((NCH, 2)), dma((NCH, 2)), dma((2 * Y - 1,)), dma((2 * Y - 1,)),
                dma((X - 1, 2)), dma((X - 1, 2)), dma((NCH, X - 1, 2)), dma((NCH, X - 1, 2)),
                dma((X - 1,)), dma((X - 1,)),
                dma((PIECES,)), dma((PIECES,)), dma((PIECES, Y - 1)), dma((PIECES, Y - 1)),
                dma((PIECES,)), dma((PIECES,)),
            ],
            compiler_params=pltpu.CompilerParams(
                collective_id=0, has_side_effects=True, vmem_limit_bytes=56 * 1024 * 1024
            ),
            name="attention_layer",
        )(inputs[0], doc_lengths, freq, w_query[0], w_key[0], w_value[0], w_out[0])
        return out[None]

    in_specs = (
        P("pipe", ("ctx", "tp"), None),
        P("pipe", None),
        P("pipe", None, "tp"),
        P("pipe", "ctx", "tp"),
        P("pipe", "ctx", "tp"),
        P("pipe", "tp", None),
    )
    out_specs = P("pipe", ("ctx", "tp"), None)
    return jax.shard_map(
        on_device, mesh=mesh, in_specs=in_specs, out_specs=out_specs, check_vma=False
    )
```

time: 514 us -> 133 us (0.26)
  the two profiles are of different devices: /device:TPU:2 before, /device:TPU:4 now
where the time goes in v1:
time: 133 us; the launch traced here: 132 us
  Pallas kernels  131 us (98%)
  local copies, waits for them, and re-layouts  1.72 us (1%)
    pallas_call x1, Pallas kernels, on_device(): pl.pallas_call(functools.partial(layer_kernel, (NP, X, Y)), out_shape=jax...  131 us

profile of v1, /device:TPU:4, one launch (start us, length us, event | category | flops | bytes accessed | tf_op | source)
XLA Modules:
  0.0 132.5 jit_solution(3112722737035907732)
XLA Ops:
  0.0 130.7 %attention_layer.1 = bf16[32,5120]{1,0:T(8,128)(2,1)} custom-call(bf16[32,5120]{1,0:T(8,128)(2,1)} %bitcast.9, s32[1,8]{1,0:T(1,128)} %len_ref.1, f32[8,128]{1,0:T(8,128)} %constant.2.clone.freq_ref, bf16[5120,384]{1,0:T(8,128)(2,1)} %bitcast.6, bf16[640,128]{1,0:T(8,128)(2,1)} %bitcast.10, bf16[640,128]{1,0:T(8,128)(2,1)} %bitcast.11, bf16[384,5120]{1,0:T(8,128)(2,1)} %bitcast.7), custom_call_target="tpu_custom_call" | custom-call | tf_op jit(solution)/shard_map/attention_layer/pallas_call | solution.py:317
  130.8 1.7 %copy.9 = bf16[1,32,5120]{2,1,0:T(8,128)(2,1)} copy(bf16[1,32,5120]{2,1,0:T(8,128)(2,1)} %bitcast.8) | data formatting | bytes 655360

commit v2 on v1

--- a/solution.py
+++ b/solution.py
@@ -12,8 +12,10 @@
 ROPE_BASE = 500000.0
 NORM_EPS = 1e-06
 ROWS = 128
-PIECES = 4
+PIECES = 8
 NEG = -1e30
+LAG = 2
+WIN = 2
 MESH = pl.DeviceIdType.MESH
 
 
@@ -91,9 +93,15 @@
         dst = (wk, wv)[i].at[rows(base + j * ROWS, ROWS)]
         return copy(src, dst, z_s.at[j, i], z_r.at[j, i], z_dev)
 
-    for j in range(NCH):
+    for j in range(WIN):
         for i in range(2):
             z_copy(j, i, mine).start()
+
+    def z_next(j):
+        if 0 <= j < NCH - WIN:
+            for i in range(2):
+                z_copy(j, i, mine).wait_send()
+                z_copy(j + WIN, i, mine).start()
 
     def tok_copy(r, who):
         return copy(x_ref, tok.at[rows(who * TR, TR)], t_s.at[r - 1], t_r.at[r - 1], (pipe, ctx, flip(t, r, TP)))
@@ -134,6 +142,8 @@
         scaled = head * lax.rsqrt(jnp.mean(head * head, axis=-1, keepdims=True) + NORM_EPS)
         return (scaled * cosb[...] + pltpu.roll(scaled, HD // 2, 1) * sinb[...]).astype(jnp.bfloat16)
 
+    for j in range(4 - WIN):
+        z_next(j)
     locals_[0].wait()
     for r in range(1, TP):
         tok_copy(r, flip(t, r, TP)).wait_recv()
@@ -157,14 +167,10 @@
             own_copy(r, i, flip(x, r, X)).wait_recv()
     kv_acc[...] = jnp.zeros_like(kv_acc)
 
-    def kv_add(start, n):
-        s = rows(start, n)
-        left = tok[:, s]
-        kv_acc[0] += jnp.dot(left, wk[s, :], preferred_element_type=jnp.float32)
-        kv_acc[1] += jnp.dot(left, wv[s, :], preferred_element_type=jnp.float32)
-
     def kv_step(i, carry):
-        kv_add((zhi * X + i) * RB, ROWS * NCH)
+        s = rows((zhi * X + i) * RB, ROWS * NCH)
+        right = jnp.concatenate([wk[s, :], wv[s, :]], axis=1)
+        kv_acc[...] += jnp.dot(tok[:, s], right, preferred_element_type=jnp.float32)
         return carry
 
     lax.fori_loop(0, X, kv_step, 0)
@@ -176,25 +182,33 @@
     def peer_base(r):
         return ((1 - zhi) * X + flip(x, r, X)) * RB
 
+    def cols_of(xx, j):
+        return rows(((1 - zhi) * X + xx) * RB + j * ROWS, ROWS)
+
     def take_chunk(j):
-        kv_add(theirs + j * ROWS, ROWS)
         for r in range(1, X):
             for i in range(2):
                 fwd_copy(j, r, i, peer_base(r)).wait_recv()
-            kv_add(peer_base(r) + j * ROWS, ROWS)
+        left = jnp.concatenate([tok[:, cols_of(r, j)] for r in range(X)], axis=1)
+        right = jnp.concatenate(
+            [jnp.concatenate([w[cols_of(r, j), :] for r in range(X)], axis=0) for w in (wk, wv)], axis=1
+        )
+        kv_acc[...] += jnp.dot(left, right, preferred_element_type=jnp.float32)
 
     for j in range(NCH):
+        z_next(4 - WIN + j)
         for i in range(2):
             z_copy(j, i, theirs).wait_recv()
         for r in range(1, X):
             for i in range(2):
                 fwd_copy(j, r, i, theirs).start()
-        if j:
+        if j and j < NCH - 1:
             take_chunk(j - 1)
+    take_chunk(NCH - 2)
     take_chunk(NCH - 1)
 
-    kvb[0, 0] = norm_rotate(kv_acc[0])
-    kvb[0, 1] = kv_acc[1].astype(jnp.bfloat16)
+    kvb[0, 0] = norm_rotate(kv_acc[:, :HD])
+    kvb[0, 1] = kv_acc[:, HD:].astype(jnp.bfloat16)
 
     def kv_copy(d, xx):
         return copy(kvb.at[0], kvb.at[d], kv_s.at[d - 1], kv_r.at[d - 1], x_dev(xx))
@@ -251,8 +265,6 @@
         a_copy(k).start()
         return carry
 
-    lax.fori_loop(0, PIECES, project, 0)
-
     def pair_sum(k, carry):
         a_copy(k).wait_recv()
         pair[k] = (part[k, c].astype(jnp.float32) + recv_a[k].astype(jnp.float32)).astype(jnp.bfloat16)
@@ -260,7 +272,9 @@
             b_copy(k, r).start()
         return carry
 
-    lax.fori_loop(0, PIECES, pair_sum, 0)
+    lax.fori_loop(0, LAG, project, 0)
+    lax.fori_loop(LAG, PIECES, lambda k, carry: pair_sum(k - LAG, project(k, carry)), 0)
+    lax.fori_loop(PIECES - LAG, PIECES, pair_sum, 0)
 
     def last_sum(k, carry):
         whole = part[k, c, y].astype(jnp.float32) + recv_a[k, y].astype(jnp.float32)
@@ -275,7 +289,8 @@
 
     for j in range(NCH):
         for i in range(2):
-            z_copy(j, i, mine).wait_send()
+            if j >= NCH - WIN:
+                z_copy(j, i, mine).wait_send()
             for r in range(1, X):
                 fwd_copy(j, r, i, theirs).wait_send()
     for r in range(1, TP):
@@ -326,7 +341,7 @@
             out_specs=hbm,
             scratch_shapes=[
                 vmem((TB, D), bf), vmem((D, QW), bf), vmem((QW, D), bf), vmem((D, HD), bf), vmem((D, HD), bf),
-                vmem((TB, QW), f32), vmem((G * TB, HD), bf), vmem((2, TB, HD), f32), vmem((X, 2, TB, HD), bf),
+                vmem((TB, QW), f32), vmem((G * TB, HD), bf), vmem((TB, 2 * HD), f32), vmem((X, 2, TB, HD), bf),
                 vmem((X, TB, TB), f32), vmem((TB, HD), f32), vmem((TB, HD), f32), vmem((G * TB, 2 * HD), f32),
                 vmem((TB, QW), bf),
                 vmem((PIECES, 2, Y, TR, CW), bf), vmem((PIECES, Y, TR, CW), bf), vmem((PIECES, Y, TR, CW), bf),

time: 133 us -> 131 us (0.985)
  the two profiles are of different devices: /device:TPU:4 before, /device:TPU:100 now
where the time goes in v2:
time: 131 us
  Pallas kernels  129 us (98%)
  local copies, waits for them, and re-layouts  1.72 us (1%)
    pallas_call x1, Pallas kernels, on_device(): pl.pallas_call(functools.partial(layer_kernel, (NP, X, Y)), out_shape=jax...  129 us

profile of v2, /device:TPU:100, one launch (start us, length us, event | category | flops | bytes accessed | tf_op | source)
XLA Modules:
  0.0 130.8 jit_solution(14127808936173965220)
XLA Ops:
  0.0 129.0 %attention_layer.1 = bf16[32,5120]{1,0:T(8,128)(2,1)} custom-call(bf16[32,5120]{1,0:T(8,128)(2,1)} %bitcast.9, s32[1,8]{1,0:T(1,128)} %len_ref.1, f32[8,128]{1,0:T(8,128)} %constant.2.clone.freq_ref, bf16[5120,384]{1,0:T(8,128)(2,1)} %bitcast.6, bf16[640,128]{1,0:T(8,128)(2,1)} %bitcast.10, bf16[640,128]{1,0:T(8,128)(2,1)} %bitcast.11, bf16[384,5120]{1,0:T(8,128)(2,1)} %bitcast.7), custom_call_target="tpu_custom_call" | custom-call | tf_op jit(solution)/shard_map/attention_layer/pallas_call | solution.py:332
  129.1 1.7 %copy.9 = bf16[1,32,5120]{2,1,0:T(8,128)(2,1)} copy(bf16[1,32,5120]{2,1,0:T(8,128)(2,1)} %bitcast.8) | data formatting | bytes 655360

commit v3 on v2

--- a/solution.py
+++ b/solution.py
@@ -24,7 +24,7 @@
     x_ref, len_ref, freq_ref, wq_ref, wk_ref, wv_ref, wo_ref,
     o_ref,
     tok, wq, wo, wk, wv, q_acc, qr, kv_acc, kvb, mask, cosb, sinb, acc, att,
-    part, recv_a, pair, recv_b, outb,
+    part, recv_a, pair, recv_b, half, outb,
     l_sem, z_s, z_r, t_s, t_r, own_s, own_r, fwd_s, fwd_r, kv_s, kv_r,
     a_s, a_r, b_s, b_r, c_s, c_r,
 ):
@@ -249,9 +249,21 @@
     def a_copy(k):
         return copy(part.at[k, 1 - c], recv_a.at[k], a_s.at[k], a_r.at[k], core_dev)
 
+    near, far = flip(y, 1, Y), flip(y, 3, Y)
+
+    def first_of(k):
+        return near + (far - near) * (k % 2)
+
+    def second_of(k):
+        return far + (near - far) * (k % 2)
+
     def b_copy(k, r):
-        yy = flip(y, r, Y)
-        return copy(pair.at[k, yy], recv_b.at[k, r - 1], b_s.at[k, r - 1], b_r.at[k, r - 1], (pipe, ctx, yy * 2 + c))
+        to = first_of(k)
+        which = flip(y, 2, Y) if r else to
+        return copy(pair.at[k, which], recv_b.at[k, r], b_s.at[k, r], b_r.at[k, r], (pipe, ctx, to * 2 + c))
+
+    def h_copy(k):
+        return copy(half.at[k], recv_b.at[k, 2], b_s.at[k, 2], b_r.at[k, 2], (pipe, ctx, second_of(k) * 2 + c))
 
     def c_copy(k):
         return copy(outb.at[k], o_ref.at[:, rows(k * CW, CW)], c_s.at[k], c_r.at[k], next_dev)
@@ -268,8 +280,16 @@
     def pair_sum(k, carry):
         a_copy(k).wait_recv()
         pair[k] = (part[k, c].astype(jnp.float32) + recv_a[k].astype(jnp.float32)).astype(jnp.bfloat16)
-        for r in range(Y - 1, 0, -1):
-            b_copy(k, r).start()
+        b_copy(k, 1).start()
+        b_copy(k, 0).start()
+        return carry
+
+    def half_sum(k, carry):
+        b_copy(k, 1).wait_recv()
+        to = second_of(k)
+        mid = part[k, c, to].astype(jnp.float32) + recv_a[k, to].astype(jnp.float32)
+        half[k] = (mid + recv_b[k, 1].astype(jnp.float32)).astype(jnp.bfloat16)
+        h_copy(k).start()
         return carry
 
     lax.fori_loop(0, LAG, project, 0)
@@ -278,14 +298,16 @@
 
     def last_sum(k, carry):
         whole = part[k, c, y].astype(jnp.float32) + recv_a[k, y].astype(jnp.float32)
-        for r in range(1, Y):
-            b_copy(k, r).wait_recv()
-            whole = whole + recv_b[k, r - 1].astype(jnp.float32)
+        b_copy(k, 0).wait_recv()
+        h_copy(k).wait_recv()
+        whole = whole + recv_b[k, 0].astype(jnp.float32) + recv_b[k, 2].astype(jnp.float32)
         outb[k] = whole.astype(jnp.bfloat16)
         c_copy(k).start()
         return carry
 
-    lax.fori_loop(0, PIECES, last_sum, 0)
+    lax.fori_loop(0, LAG, half_sum, 0)
+    lax.fori_loop(LAG, PIECES, lambda k, carry: last_sum(k - LAG, half_sum(k, carry)), 0)
+    lax.fori_loop(PIECES - LAG, PIECES, last_sum, 0)
 
     for j in range(NCH):
         for i in range(2):
@@ -306,8 +328,9 @@
 
     def drain(k, carry):
         a_copy(k).wait_send()
-        for r in range(1, Y):
-            b_copy(k, r).wait_send()
+        b_copy(k, 0).wait_send()
+        b_copy(k, 1).wait_send()
+        h_copy(k).wait_send()
         c_copy(k).wait_send()
         c_copy(k).wait_recv()
         return carry
@@ -345,7 +368,7 @@
                 vmem((X, TB, TB), f32), vmem((TB, HD), f32), vmem((TB, HD), f32), vmem((G * TB, 2 * HD), f32),
                 vmem((TB, QW), bf),
                 vmem((PIECES, 2, Y, TR, CW), bf), vmem((PIECES, Y, TR, CW), bf), vmem((PIECES, Y, TR, CW), bf),
-                vmem((PIECES, Y - 1, TR, CW), bf), vmem((PIECES, TR, CW), bf),
+                vmem((PIECES, Y - 1, TR, CW), bf), vmem((PIECES, TR, CW), bf), vmem((PIECES, TR, CW), bf),
                 dma((5,)), dma((NCH, 2)), dma((NCH, 2)), dma((2 * Y - 1,)), dma((2 * Y - 1,)),
                 dma((X - 1, 2)), dma((X - 1, 2)), dma((NCH, X - 1, 2)), dma((NCH, X - 1, 2)),
                 dma((X - 1,)), dma((X - 1,)),

time: 131 us -> 132 us (level)
  the two profiles are of different devices: /device:TPU:100 before, /device:TPU:102 now
where the time goes in v3:
time: 132 us
  Pallas kernels  130 us (98%)
  local copies, waits for them, and re-layouts  1.72 us (1%)
    pallas_call x1, Pallas kernels, on_device(): pl.pallas_call(functools.partial(layer_kernel, (NP, X, Y)), out_shape=jax...  130 us

profile of v3, /device:TPU:102, one launch (start us, length us, event | category | flops | bytes accessed | tf_op | source)
XLA Modules:
  0.0 131.7 jit_solution(9658214579955204390)
XLA Ops:
  0.0 130.0 %attention_layer.1 = bf16[32,5120]{1,0:T(8,128)(2,1)} custom-call(bf16[32,5120]{1,0:T(8,128)(2,1)} %bitcast.9, s32[1,8]{1,0:T(1,128)} %len_ref.1, f32[8,128]{1,0:T(8,128)} %constant.2.clone.freq_ref, bf16[5120,384]{1,0:T(8,128)(2,1)} %bitcast.6, bf16[640,128]{1,0:T(8,128)(2,1)} %bitcast.10, bf16[640,128]{1,0:T(8,128)(2,1)} %bitcast.11, bf16[384,5120]{1,0:T(8,128)(2,1)} %bitcast.7), custom_call_target="tpu_custom_call" | custom-call | tf_op jit(solution)/shard_map/attention_layer/pallas_call | solution.py:355
  130.0 1.7 %copy.9 = bf16[1,32,5120]{2,1,0:T(8,128)(2,1)} copy(bf16[1,32,5120]{2,1,0:T(8,128)(2,1)} %bitcast.8) | data formatting | bytes 655360

commit v4 on v2

--- a/solution.py
+++ b/solution.py
@@ -313,6 +313,24 @@
         return carry
 
     lax.fori_loop(0, PIECES, drain, 0)
+
+
+def deliver(src_ref, dst_ref, held, in_sem, out_sem):
+    BR = 8
+    count = src_ref.shape[0] // BR
+    taken = [
+        pltpu.make_async_copy(src_ref.at[pl.ds(i * BR, BR)], held.at[i], in_sem.at[i]) for i in range(count)
+    ]
+    given = [
+        pltpu.make_async_copy(held.at[i], dst_ref.at[pl.ds(i * BR, BR)], out_sem.at[i]) for i in range(count)
+    ]
+    for cp in taken:
+        cp.start()
+    for i in range(count):
+        taken[i].wait()
+        given[i].start()
+    for cp in given:
+        cp.wait()
 
 
 def solution(mesh):
@@ -357,6 +375,14 @@
             ),
             name="attention_layer",
         )(inputs[0], doc_lengths, freq, w_query[0], w_key[0], w_value[0], w_out[0])
+        out = pl.pallas_call(
+            deliver,
+            out_shape=jax.ShapeDtypeStruct((TR, D), bf),
+            in_specs=[hbm],
+            out_specs=hbm,
+            scratch_shapes=[vmem((TR // 8, 8, D), bf), dma((TR // 8,)), dma((TR // 8,))],
+            name="deliver",
+        )(out)
         return out[None]
 
     in_specs = (

time: 131 us -> 131 us (level)
  Pallas kernels: 129 us -> 131 us
  local copies, waits for them, and re-layouts: 1.72 us -> 0 us
    unnamed x1 -> x0, local copies, waits for them, and re-layouts: 1.72 us -> none
    pallas_call x0 -> x1, Pallas kernels: none -> 1.71 us  [on_device(): pl.pallas_call(deliver, out_shape=jax.ShapeDtypeStruct((TR, D), bf), in_s...]
where the time goes in v4:
time: 131 us
  Pallas kernels  131 us (100%)
    pallas_call x1, Pallas kernels, on_device(): pl.pallas_call(functools.partial(layer_kernel, (NP, X, Y)), out_shape=jax...  129 us

profile of v4, /device:TPU:100, one launch (start us, length us, event | category | flops | bytes accessed | tf_op | source)
XLA Modules:
  0.0 130.8 jit_solution(47317091912872490)
XLA Ops:
  0.0 129.0 %attention_layer.1.src_ref = bf16[32,5120]{1,0:T(8,128)(2,1)} custom-call(bf16[32,5120]{1,0:T(8,128)(2,1)} %bitcast.8, s32[1,8]{1,0:T(1,128)} %len_ref.1, f32[8,128]{1,0:T(8,128)} %constant.2.clone.freq_ref, bf16[5120,384]{1,0:T(8,128)(2,1)} %bitcast.6, bf16[640,128]{1,0:T(8,128)(2,1)} %bitcast.9, bf16[640,128]{1,0:T(8,128)(2,1)} %bitcast.10, ...), custom_call_target="tpu_custom_call" | custom-call | tf_op jit(solution)/shard_map/attention_layer/pallas_call | solution.py:350
  129.1 1.7 %deliver.1 = bf16[32,5120]{1,0:T(8,128)(2,1)} custom-call(bf16[32,5120]{1,0:T(8,128)(2,1)} %attention_layer.1.src_ref), custom_call_target="tpu_custom_call" | custom-call | tf_op jit(solution)/shard_map/deliver/pallas_call | solution.py:378
